TPU v7x, 256 devices: a whole 4x4x8 slice. The times are simulated.
256 devices in a mesh: dp: 8 (over y, core), ctx: 32 (over z, x).
Axes of the slice: x: 4, y: 4, z: 8, core: 2. Of those that a mesh axis runs over, the one named last changes fastest.
Arguments:
- q_in: bfloat16 [65536, 1024], P(('dp', 'ctx')), may hold values from -5 to 5
- k_in: bfloat16 [65536, 1024], P(('dp', 'ctx')), may hold values from -5 to 5
- v_in: bfloat16 [65536, 1024], P(('dp', 'ctx')), may hold values from -6 to 6
- cotangent: bfloat16 [65536, 2048], P(('dp', 'ctx')), may hold values from -1.796875 to 1.796875
- out_weight: bfloat16 [1024, 2048], replicated, may hold values from -0.1875 to 0.1875
- cluster_ids: int32 [8, 65536, 1], P(None, ('dp', 'ctx')), may hold values from 0 to 63; in each aligned block of 256 rows (0 to 255, 256 to 511, ..., all dimensions but the last counted through in order) at most 8 rows name the same one
Outputs:
- layer_out: bfloat16 [65536, 2048], P(('dp', 'ctx'))
- q_grad: bfloat16 [65536, 1024], P(('dp', 'ctx'))
- k_grad: bfloat16 [65536, 1024], P(('dp', 'ctx'))
- v_grad: bfloat16 [65536, 1024], P(('dp', 'ctx'))
- wo_grad: float32 [1024, 2048], P('ctx')
Inputs may be any that keep to these rules, and one draw needn't show every extreme that they name: `cluster_ids`: for each head, the 256 tokens of one device name any one cluster at most 8 times, a bound that some block reaches.
All inputs are finite; a program needn't handle non-finite values.
Results may differ from a plain program's by a relative error of at most 0.0085.
Values may be sent and summed in bfloat16 or wider, within the bound.
No kernel may reach another device: no remote copies, remote signals or barrier semaphores. Data moves between devices by JAX's collectives and lax.ppermute only.
A program may use at most 128 MiB of HBM per device.

v0:
```python
import math
import jax
import jax.numpy as jnp
from jax import lax
from jax.sharding import PartitionSpec as P

HEADS = 8
HEAD_DIM = 128
C_DEV = 2
SEQS = 1
NEG_FILL = -1e30


def attend_groups(query, keys_in, values_in, grad_out, position, filled, seq_length):
    score_scale = HEAD_DIM ** (-0.5)
    scores = (
        jnp.einsum("grd,gsd->grs", query, keys_in, preferred_element_type=jnp.float32) * score_scale
    )
    sequence = position // seq_length
    allowed = (
        filled[:, :, None]
        & filled[:, None, :]
        & (position[:, None, :] <= position[:, :, None])
        & (sequence[:, None, :] == sequence[:, :, None])
    )
    scores = jnp.where(allowed, scores, NEG_FILL)
    row_peak = jnp.max(scores, axis=-1, keepdims=True)
    exp_terms = jnp.exp(scores - row_peak)
    weights = exp_terms / jnp.sum(exp_terms, axis=-1, keepdims=True)
    weights_low = weights.astype(jnp.bfloat16)
    attended = jnp.einsum(
        "grs,gsd->grd", weights_low, values_in, preferred_element_type=jnp.float32
    ).astype(jnp.bfloat16)
    grad_prob = jnp.einsum("grd,gsd->grs", grad_out, values_in, preferred_element_type=jnp.float32)
    row_delta = jnp.sum(weights * grad_prob, axis=-1, keepdims=True)
    grad_score = (weights * (grad_prob - row_delta) * score_scale).astype(jnp.bfloat16)
    query_grad = jnp.einsum(
        "grs,gsd->grd", grad_score, keys_in, preferred_element_type=jnp.float32
    ).astype(jnp.bfloat16)
    key_grad = jnp.einsum(
        "grs,grd->gsd", grad_score, query, preferred_element_type=jnp.float32
    ).astype(jnp.bfloat16)
    value_grad = jnp.einsum(
        "grs,grd->gsd", weights_low, grad_out, preferred_element_type=jnp.float32
    ).astype(jnp.bfloat16)
    return (attended, query_grad, key_grad, value_grad)


def per_device(q_in, k_in, v_in, cotangent, out_weight, cluster_ids):
    ctx_size = lax.axis_size("ctx")
    dp_size = lax.axis_size("dp")
    tok_count = q_in.shape[0]
    clusters = C_DEV * ctx_size
    capacity = 2 * tok_count // clusters
    seq_length = tok_count * ctx_size // SEQS
    tok_iota = jnp.arange(tok_count, dtype=jnp.int32)
    lower_ones = (tok_iota[:, None] >= tok_iota[None, :]).astype(jnp.bfloat16)
    local_ids = cluster_ids[:, :, 0]
    cluster_hits = (local_ids[:, :, None] == jnp.arange(clusters, dtype=jnp.int32)).astype(
        jnp.bfloat16
    )
    running = jnp.einsum(
        "tu,huc->htc", lower_ones, cluster_hits, preferred_element_type=jnp.float32
    )
    rank_in_block = (jnp.sum(running * cluster_hits, axis=-1) - 1.0).astype(jnp.int32)
    slot_index = local_ids * capacity + rank_in_block
    dispatch = (slot_index[:, :, None] == jnp.arange(clusters * capacity, dtype=jnp.int32)).astype(
        jnp.bfloat16
    )
    grad_heads = lax.dot_general(
        cotangent, out_weight, (((1,), (1,)), ((), ())), preferred_element_type=jnp.float32
    ).astype(jnp.bfloat16)

    def to_slots(token_rows):
        per_head = token_rows.reshape(tok_count, HEADS, HEAD_DIM)
        slotted = jnp.einsum("hts,thd->hsd", dispatch, per_head, preferred_element_type=jnp.float32)
        return slotted.astype(jnp.bfloat16).reshape(HEADS, ctx_size, C_DEV, capacity, HEAD_DIM)

    query_slots = to_slots(q_in)
    key_slots = to_slots(k_in)
    value_slots = to_slots(v_in)
    grad_slots = to_slots(grad_heads)
    pieces = []
    for head_index in range(HEADS):
        pieces.append(
            (
                lax.all_to_all(
                    query_slots[head_index], "ctx", split_axis=0, concat_axis=2, tiled=True
                ),
                lax.all_to_all(
                    key_slots[head_index], "ctx", split_axis=0, concat_axis=2, tiled=True
                ),
                lax.all_to_all(
                    value_slots[head_index], "ctx", split_axis=0, concat_axis=2, tiled=True
                ),
                lax.all_to_all(
                    grad_slots[head_index], "ctx", split_axis=0, concat_axis=2, tiled=True
                ),
            )
        )
    arrived = tuple(
        (jnp.stack([piece_set[member_index] for piece_set in pieces]) for member_index in range(4))
    )
    group_count = C_DEV
    group_rows = ctx_size * capacity
    every_ids = lax.all_gather(cluster_ids, "ctx", axis=1, tiled=True)
    source_ids = every_ids[:, :, 0].reshape(HEADS, ctx_size, tok_count)
    owner_index = lax.axis_index("ctx")
    owned_hits = (
        source_ids[..., None] == owner_index * C_DEV + jnp.arange(C_DEV, dtype=jnp.int32)
    ).astype(jnp.bfloat16)
    owned_running = jnp.einsum(
        "tu,hsuc->hstc", lower_ones, owned_hits, preferred_element_type=jnp.float32
    )
    owned_rank = (owned_running - 1.0).astype(jnp.int32)
    slot_match = (owned_hits[..., None] > 0) & (
        owned_rank[..., None] == jnp.arange(capacity, dtype=jnp.int32)
    )
    filled = jnp.any(slot_match, axis=2)
    token_at = jnp.sum(jnp.where(slot_match, tok_iota[None, None, :, None, None], 0), axis=2)
    position = jnp.arange(ctx_size, dtype=jnp.int32)[None, :, None, None] * tok_count + token_at
    position = position.transpose(0, 2, 1, 3).reshape(HEADS, group_count, group_rows)
    filled = filled.transpose(0, 2, 1, 3).reshape(HEADS, group_count, group_rows)

    def group_view(received):
        return received.reshape(HEADS, group_count, group_rows, HEAD_DIM)

    def head_work(operands):
        return attend_groups(
            operands[0], operands[1], operands[2], operands[3], operands[4], operands[5], seq_length
        )

    attended, query_grad, key_grad, value_grad = lax.map(
        head_work,
        (
            group_view(arrived[0]),
            group_view(arrived[1]),
            group_view(arrived[2]),
            group_view(arrived[3]),
            position,
            filled,
        ),
    )

    def owner_view(result):
        return result.reshape(HEADS, 1, C_DEV, ctx_size * capacity, HEAD_DIM)

    returned = (
        lax.all_to_all(owner_view(attended), "ctx", split_axis=3, concat_axis=1, tiled=True),
        lax.all_to_all(owner_view(query_grad), "ctx", split_axis=3, concat_axis=1, tiled=True),
        lax.all_to_all(owner_view(key_grad), "ctx", split_axis=3, concat_axis=1, tiled=True),
        lax.all_to_all(owner_view(value_grad), "ctx", split_axis=3, concat_axis=1, tiled=True),
    )

    def from_slots(slotted):
        flat = slotted.reshape(HEADS, clusters * capacity, HEAD_DIM)
        token_rows = jnp.einsum("hts,hsd->thd", dispatch, flat, preferred_element_type=jnp.float32)
        return token_rows.astype(jnp.bfloat16).reshape(tok_count, HEADS * HEAD_DIM)

    attn_out = from_slots(returned[0])
    q_grad = from_slots(returned[1])
    k_grad = from_slots(returned[2])
    v_grad = from_slots(returned[3])
    layer_out = jnp.dot(attn_out, out_weight, preferred_element_type=jnp.float32).astype(
        jnp.bfloat16
    )
    grad_factor = 1.0 / math.sqrt(tok_count * ctx_size * dp_size)
    shard_sum = lax.psum_scatter(
        lax.dot_general(
            attn_out, cotangent, (((0,), (0,)), ((), ())), preferred_element_type=jnp.float32
        )
        * grad_factor,
        "ctx",
        scatter_dimension=0,
        tiled=True,
    )
    wo_grad = lax.psum(shard_sum, "dp")
    return (layer_out, q_grad, k_grad, v_grad, wo_grad)


def solution(mesh):
    placed = (
        P(("dp", "ctx"), None),
        P(("dp", "ctx"), None),
        P(("dp", "ctx"), None),
        P(("dp", "ctx"), None),
        P(),
        P(None, ("dp", "ctx"), None),
    )
    return jax.shard_map(
        per_device,
        mesh=mesh,
        in_specs=placed,
        out_specs=(
            P(("dp", "ctx"), None),
            P(("dp", "ctx"), None),
            P(("dp", "ctx"), None),
            P(("dp", "ctx"), None),
            P("ctx", None),
        ),
        check_vma=False,
    )
```

profile of v0, /device:TPU:2, one launch (start us, length us, event | category | flops | bytes accessed | tf_op | source)
XLA Modules:
  0.0 985.0 jit_solution(15068401395105552438)
XLA Ops:
  15.1 20.5 %all_to_all.540 = bf16[32,2,8,128]{3,2,1,0:T(8,128)(2,1)} all-to-all(bf16[32,2,8,128]{3,2,1,0:T(8,128)(2,1)S(1)} %bitcast.463), channel_id=1, replica_groups=mesh['dp'=8,'ctx'=32] {'ctx'}, dimensions={0} | all-to-all | bytes 262144 | tf_op jit(solution)/shard_map/all_to_all | solution.py:96
  35.6 14.1 %all_to_all.541 = bf16[32,2,8,128]{3,2,1,0:T(8,128)(2,1)} all-to-all(bf16[32,2,8,128]{3,2,1,0:T(8,128)(2,1)S(1)} %bitcast.461), channel_id=1, replica_groups=mesh['dp'=8,'ctx'=32] {'ctx'}, dimensions={0} | all-to-all | bytes 262144 | tf_op jit(solution)/shard_map/all_to_all | solution.py:96
  49.7 14.3 %all_to_all.542 = bf16[32,2,8,128]{3,2,1,0:T(8,128)(2,1)} all-to-all(bf16[32,2,8,128]{3,2,1,0:T(8,128)(2,1)S(1)} %bitcast.460), channel_id=1, replica_groups=mesh['dp'=8,'ctx'=32] {'ctx'}, dimensions={0} | all-to-all | bytes 262144 | tf_op jit(solution)/shard_map/all_to_all | solution.py:96
  64.0 14.2 %all_to_all.543 = bf16[32,2,8,128]{3,2,1,0:T(8,128)(2,1)} all-to-all(bf16[32,2,8,128]{3,2,1,0:T(8,128)(2,1)S(1)} %bitcast.459), channel_id=1, replica_groups=mesh['dp'=8,'ctx'=32] {'ctx'}, dimensions={0} | all-to-all | bytes 262144 | tf_op jit(solution)/shard_map/all_to_all | solution.py:96
  78.1 14.2 %all_to_all.544 = bf16[32,2,8,128]{3,2,1,0:T(8,128)(2,1)} all-to-all(bf16[32,2,8,128]{3,2,1,0:T(8,128)(2,1)S(1)} %bitcast.458), channel_id=1, replica_groups=mesh['dp'=8,'ctx'=32] {'ctx'}, dimensions={0} | all-to-all | bytes 262144 | tf_op jit(solution)/shard_map/all_to_all | solution.py:96
  92.3 14.2 %all_to_all.545 = bf16[32,2,8,128]{3,2,1,0:T(8,128)(2,1)} all-to-all(bf16[32,2,8,128]{3,2,1,0:T(8,128)(2,1)S(1)} %bitcast.457), channel_id=1, replica_groups=mesh['dp'=8,'ctx'=32] {'ctx'}, dimensions={0} | all-to-all | bytes 262144 | tf_op jit(solution)/shard_map/all_to_all | solution.py:96
  127.4 8.0 all-to-all-done.24
  140.9 43.9 %all_gather.3 = s32[8,8192,1]{1,2,0:T(1,128)S(1)} all-gather(s32[8,256,1]{1,2,0:T(1,128)S(1)} %copy-done.20), channel_id=1, replica_groups=mesh['dp'=8,'ctx'=32] {'ctx'}, dimensions={1}, use_global_device_ids=true | all-gather | bytes 270336 | tf_op jit(solution)/shard_map/all_gather | solution.py:106
  185.5 8.7 all-to-all-start.23
  209.5 9.1 select_reduce_fusion
  218.6 9.9 %all-to-all-start.20 = ((bf16[32,2,8,128]{3,2,1,0:T(8,128)(2,1)}), bf16[32,2,8,128]{3,2,1,0:T(8,128)(2,1)S(1)}, u32[]{:S(2)}, u32[]{:S(2)}) async-start(bf16[32,2,8,128]{3,2,1,0:T(8,128)(2,1)} %bitcast.99), calls=%async_computation.20 | async-start | bytes 262144 | tf_op jit(solution)/shard_map/all_to_all | solution.py:93
  228.7 8.7 all-to-all-done.20
  288.3 8.0 all-to-all-done.16
  296.4 14.8 %all-to-all-start.8 = ((bf16[32,2,8,128]{3,2,1,0:T(8,128)(2,1)}), bf16[32,2,8,128]{3,2,1,0:T(8,128)(2,1)}, u32[]{:S(2)}, u32[]{:S(2)}) async-start(bf16[32,2,8,128]{3,2,1,0:T(8,128)(2,1)} %bitcast.50), calls=%async_computation.8 | async-start | bytes 262144 | tf_op jit(solution)/shard_map/all_to_all | solution.py:90
  311.2 9.1 fusion.71
  322.9 9.9 %all-to-all-start = ((bf16[32,2,8,128]{3,2,1,0:T(8,128)(2,1)}), bf16[32,2,8,128]{3,2,1,0:T(8,128)(2,1)S(1)}, u32[]{:S(2)}, u32[]{:S(2)}) async-start(bf16[32,2,8,128]{3,2,1,0:T(8,128)(2,1)} %bitcast.17), calls=%async_computation | async-start | bytes 262144 | tf_op jit(solution)/shard_map/all_to_all | solution.py:87
  478.9 8.4 all-to-all-done.2
  545.9 85.9 %while.18 = (s32[]{:T(128)}, bf16[8,2,256,128]{3,1,0,2:T(2,128)(2,1)}, bf16[8,2,256,128]{3,1,0,2:T(2,128)(2,1)}, bf16[8,2,256,128]{3,1,0,2:T(2,128)(2,1)}, bf16[...) while((s32[]{:T(128)}, ...), condition=%wide.region_7.8_spmd, body=%wide.region_3.7_spmd.sunk | while | flops 205137152 | bytes 11052245 | solution.py:133
  631.8 28.9 %all_to_all.546 = bf16[8,1,2,256,128]{4,2,0,1,3:T(2,128)(2,1)S(1)} all-to-all(bf16[8,1,2,256,128]{4,2,0,1,3:T(2,128)(2,1)} %bitcast.450), channel_id=1, replica_groups=mesh['dp'=8,'ctx'=32] {'ctx'}, dimensions={3} | all-to-all | bytes 2097152 | tf_op jit(solution)/shard_map/all_to_all | solution.py:149
  668.0 39.7 %all_to_all.547 = bf16[8,1,2,256,128]{4,2,0,1,3:T(2,128)(2,1)} all-to-all(bf16[8,1,2,256,128]{4,2,0,1,3:T(2,128)(2,1)S(1)} %bitcast.447), channel_id=1, replica_groups=mesh['dp'=8,'ctx'=32] {'ctx'}, dimensions={3} | all-to-all | bytes 2097152 | tf_op jit(solution)/shard_map/all_to_all | solution.py:152
  707.7 28.6 %all_to_all.548 = bf16[8,1,2,256,128]{4,2,0,1,3:T(2,128)(2,1)S(1)} all-to-all(bf16[8,1,2,256,128]{4,2,0,1,3:T(2,128)(2,1)S(1)} %bitcast.449), channel_id=1, replica_groups=mesh['dp'=8,'ctx'=32] {'ctx'}, dimensions={3} | all-to-all | bytes 2097152 | tf_op jit(solution)/shard_map/all_to_all | solution.py:150
  746.3 18.9 %all-to-all-done.34 = bf16[8,1,2,256,128]{4,2,0,1,3:T(2,128)(2,1)S(1)} async-done(((bf16[8,1,2,256,128]{4,2,0,1,3:T(2,128)(2,1)}), bf16[8,1,2,256,128]{4,2,0,1,3:T(2,128)(2,1)S(1)}, u32[]{:S(2)}, u32[]{:S(2)}) %all-to-all-start.34) | async-done | bytes 1048608 | tf_op jit(solution)/shard_map/all_to_all | solution.py:151
  771.4 137.6 %reduce-scatter.2.cloned.1.call-done = f32[32,2048]{1,0:T(8,128)} async-done(((f32[1024,2048]{1,0:T(8,128)}), f32[32,2048]{1,0:T(8,128)}) %reduce-scatter.2.cloned.1.call-update) | async-done | bytes 262160 | tf_op jit(solution)/shard_map/reduce_scatter | solution.py:168
  915.2 60.9 %all-reduce.2.cloned.1.call-done = f32[32,2048]{1,0:T(8,128)} async-done(((f32[32,2048]{1,0:T(8,128)}), f32[32,2048]{1,0:T(8,128)}) %all-reduce.2.cloned.1.call-update) | async-done | bytes 262160 | tf_op jit(solution)/shard_map/psum | solution.py:177
  (294 shorter events, 424.8 us)
Async XLA Ops:
  106.6 14.4 %all-to-all-start.25 = ((bf16[32,2,8,128]{3,2,1,0:T(8,128)(2,1)}), bf16[32,2,8,128]{3,2,1,0:T(8,128)(2,1)S(1)}, u32[]{:S(2)}, u32[]{:S(2)}) async-start(bf16[32,2,8,128]{3,2,1,0:T(8,128)(2,1)} %bitcast.120), calls=%async_computation.25 | async-start | bytes 262144 | tf_op jit(solution)/shard_map/all_to_all | solution.py:96
  121.0 14.4 %all-to-all-start.24 = ((bf16[32,2,8,128]{3,2,1,0:T(8,128)(2,1)}), bf16[32,2,8,128]{3,2,1,0:T(8,128)(2,1)S(1)}, u32[]{:S(2)}, u32[]{:S(2)}) async-start(bf16[32,2,8,128]{3,2,1,0:T(8,128)(2,1)} %bitcast.116), calls=%async_computation.24 | async-start | bytes 262144 | tf_op jit(solution)/shard_map/all_to_all | solution.py:96
  135.4 50.1 %all-to-all-start.22 = ((bf16[32,2,8,128]{3,2,1,0:T(8,128)(2,1)}), bf16[32,2,8,128]{3,2,1,0:T(8,128)(2,1)S(1)}, u32[]{:S(2)}, u32[]{:S(2)}) async-start(bf16[32,2,8,128]{3,2,1,0:T(8,128)(2,1)} %bitcast.107), calls=%async_computation.22 | async-start | bytes 262144 | tf_op jit(solution)/shard_map/all_to_all | solution.py:93
  185.5 17.5 %all-to-all-start.23 = ((bf16[32,2,8,128]{3,2,1,0:T(8,128)(2,1)}), bf16[32,2,8,128]{3,2,1,0:T(8,128)(2,1)S(1)}, u32[]{:S(2)}, u32[]{:S(2)}) async-start(bf16[32,2,8,128]{3,2,1,0:T(8,128)(2,1)} %bitcast.111), calls=%async_computation.23 | async-start | bytes 262144 | tf_op jit(solution)/shard_map/all_to_all | solution.py:93
  203.7 14.9 %all-to-all-start.21 = ((bf16[32,2,8,128]{3,2,1,0:T(8,128)(2,1)}), bf16[32,2,8,128]{3,2,1,0:T(8,128)(2,1)S(1)}, u32[]{:S(2)}, u32[]{:S(2)}) async-start(bf16[32,2,8,128]{3,2,1,0:T(8,128)(2,1)} %bitcast.103), calls=%async_computation.21 | async-start | bytes 262144 | tf_op jit(solution)/shard_map/all_to_all | solution.py:93
  218.6 18.8 %all-to-all-start.20 = ((bf16[32,2,8,128]{3,2,1,0:T(8,128)(2,1)}), bf16[32,2,8,128]{3,2,1,0:T(8,128)(2,1)S(1)}, u32[]{:S(2)}, u32[]{:S(2)}) async-start(bf16[32,2,8,128]{3,2,1,0:T(8,128)(2,1)} %bitcast.99), calls=%async_computation.20 | async-start | bytes 262144 | tf_op jit(solution)/shard_map/all_to_all | solution.py:93
  251.7 14.4 %all-to-all-start.18 = ((bf16[32,2,8,128]{3,2,1,0:T(8,128)(2,1)}), bf16[32,2,8,128]{3,2,1,0:T(8,128)(2,1)S(1)}, u32[]{:S(2)}, u32[]{:S(2)}) async-start(bf16[32,2,8,128]{3,2,1,0:T(8,128)(2,1)} %bitcast.91), calls=%async_computation.18 | async-start | bytes 262144 | tf_op jit(solution)/shard_map/all_to_all | solution.py:93
  266.2 15.1 %all-to-all-start.17 = ((bf16[32,2,8,128]{3,2,1,0:T(8,128)(2,1)}), bf16[32,2,8,128]{3,2,1,0:T(8,128)(2,1)}, u32[]{:S(2)}, u32[]{:S(2)}) async-start(bf16[32,2,8,128]{3,2,1,0:T(8,128)(2,1)} %bitcast.87), calls=%async_computation.17 | async-start | bytes 262144 | tf_op jit(solution)/shard_map/all_to_all | solution.py:93
  281.3 15.1 %all-to-all-start.16 = ((bf16[32,2,8,128]{3,2,1,0:T(8,128)(2,1)}), bf16[32,2,8,128]{3,2,1,0:T(8,128)(2,1)}, u32[]{:S(2)}, u32[]{:S(2)}) async-start(bf16[32,2,8,128]{3,2,1,0:T(8,128)(2,1)} %bitcast.83), calls=%async_computation.16 | async-start | bytes 262144 | tf_op jit(solution)/shard_map/all_to_all | solution.py:93
  296.4 26.5 %all-to-all-start.8 = ((bf16[32,2,8,128]{3,2,1,0:T(8,128)(2,1)}), bf16[32,2,8,128]{3,2,1,0:T(8,128)(2,1)}, u32[]{:S(2)}, u32[]{:S(2)}) async-start(bf16[32,2,8,128]{3,2,1,0:T(8,128)(2,1)} %bitcast.50), calls=%async_computation.8 | async-start | bytes 262144 | tf_op jit(solution)/shard_map/all_to_all | solution.py:90
  322.9 18.8 %all-to-all-start = ((bf16[32,2,8,128]{3,2,1,0:T(8,128)(2,1)}), bf16[32,2,8,128]{3,2,1,0:T(8,128)(2,1)S(1)}, u32[]{:S(2)}, u32[]{:S(2)}) async-start(bf16[32,2,8,128]{3,2,1,0:T(8,128)(2,1)} %bitcast.17), calls=%async_computation | async-start | bytes 262144 | tf_op jit(solution)/shard_map/all_to_all | solution.py:87
  341.7 14.5 %all-to-all-start.14 = ((bf16[32,2,8,128]{3,2,1,0:T(8,128)(2,1)}), bf16[32,2,8,128]{3,2,1,0:T(8,128)(2,1)S(1)}, u32[]{:S(2)}, u32[]{:S(2)}) async-start(bf16[32,2,8,128]{3,2,1,0:T(8,128)(2,1)} %bitcast.74), calls=%async_computation.14 | async-start | bytes 262144 | tf_op jit(solution)/shard_map/all_to_all | solution.py:90
  370.6 14.4 %all-to-all-start.13 = ((bf16[32,2,8,128]{3,2,1,0:T(8,128)(2,1)}), bf16[32,2,8,128]{3,2,1,0:T(8,128)(2,1)S(1)}, u32[]{:S(2)}, u32[]{:S(2)}) async-start(bf16[32,2,8,128]{3,2,1,0:T(8,128)(2,1)} %bitcast.70), calls=%async_computation.13 | async-start | bytes 262144 | tf_op jit(solution)/shard_map/all_to_all | solution.py:90
  385.0 14.6 %all-to-all-start.12 = ((bf16[32,2,8,128]{3,2,1,0:T(8,128)(2,1)}), bf16[32,2,8,128]{3,2,1,0:T(8,128)(2,1)S(1)}, u32[]{:S(2)}, u32[]{:S(2)}) async-start(bf16[32,2,8,128]{3,2,1,0:T(8,128)(2,1)} %bitcast.66), calls=%async_computation.12 | async-start | bytes 262144 | tf_op jit(solution)/shard_map/all_to_all | solution.py:90
  428.4 14.5 %all-to-all-start.9 = ((bf16[32,2,8,128]{3,2,1,0:T(8,128)(2,1)}), bf16[32,2,8,128]{3,2,1,0:T(8,128)(2,1)S(1)}, u32[]{:S(2)}, u32[]{:S(2)}) async-start(bf16[32,2,8,128]{3,2,1,0:T(8,128)(2,1)} %bitcast.54), calls=%async_computation.9 | async-start | bytes 262144 | tf_op jit(solution)/shard_map/all_to_all | solution.py:90
  457.3 14.5 %all-to-all-start.4 = ((bf16[32,2,8,128]{3,2,1,0:T(8,128)(2,1)}), bf16[32,2,8,128]{3,2,1,0:T(8,128)(2,1)S(1)}, u32[]{:S(2)}, u32[]{:S(2)}) async-start(bf16[32,2,8,128]{3,2,1,0:T(8,128)(2,1)} %bitcast.33), calls=%async_computation.4 | async-start | bytes 262144 | tf_op jit(solution)/shard_map/all_to_all | solution.py:87
  471.8 15.5 %all-to-all-start.2 = ((bf16[32,2,8,128]{3,2,1,0:T(8,128)(2,1)}), bf16[32,2,8,128]{3,2,1,0:T(8,128)(2,1)S(1)}, u32[]{:S(2)}, u32[]{:S(2)}) async-start(bf16[32,2,8,128]{3,2,1,0:T(8,128)(2,1)} %bitcast.25), calls=%async_computation.2 | async-start | bytes 262144 | tf_op jit(solution)/shard_map/all_to_all | solution.py:87
  487.3 14.7 %all-to-all-start.1 = ((bf16[32,2,8,128]{3,2,1,0:T(8,128)(2,1)}), bf16[32,2,8,128]{3,2,1,0:T(8,128)(2,1)S(1)}, u32[]{:S(2)}, u32[]{:S(2)}) async-start(bf16[32,2,8,128]{3,2,1,0:T(8,128)(2,1)} %bitcast.21), calls=%async_computation.1 | async-start | bytes 262144 | tf_op jit(solution)/shard_map/all_to_all | solution.py:87
  502.0 14.4 %all-to-all-start.3 = ((bf16[32,2,8,128]{3,2,1,0:T(8,128)(2,1)}), bf16[32,2,8,128]{3,2,1,0:T(8,128)(2,1)S(1)}, u32[]{:S(2)}, u32[]{:S(2)}) async-start(bf16[32,2,8,128]{3,2,1,0:T(8,128)(2,1)} %bitcast.29), calls=%async_computation.3 | async-start | bytes 262144 | tf_op jit(solution)/shard_map/all_to_all | solution.py:87
  516.4 14.4 %all-to-all-start.5 = ((bf16[32,2,8,128]{3,2,1,0:T(8,128)(2,1)}), bf16[32,2,8,128]{3,2,1,0:T(8,128)(2,1)S(1)}, u32[]{:S(2)}, u32[]{:S(2)}) async-start(bf16[32,2,8,128]{3,2,1,0:T(8,128)(2,1)} %bitcast.37), calls=%async_computation.5 | async-start | bytes 262144 | tf_op jit(solution)/shard_map/all_to_all | solution.py:87
  530.9 14.4 %all-to-all-start.7 = ((bf16[32,2,8,128]{3,2,1,0:T(8,128)(2,1)}), bf16[32,2,8,128]{3,2,1,0:T(8,128)(2,1)S(1)}, u32[]{:S(2)}, u32[]{:S(2)}) async-start(bf16[32,2,8,128]{3,2,1,0:T(8,128)(2,1)} %bitcast.45), calls=%async_computation.7 | async-start | bytes 262144 | tf_op jit(solution)/shard_map/all_to_all | solution.py:87
  536.3 372.7 %reduce-scatter.2.cloned.1.call-start = ((), (), s32[]{:S(2)}) async-start(), calls=%async_computation.37 | async-start | bytes 8650752 | tf_op jit(solution)/shard_map/reduce_scatter | solution.py:168
  736.3 28.9 %all-to-all-start.34 = ((bf16[8,1,2,256,128]{4,2,0,1,3:T(2,128)(2,1)}), bf16[8,1,2,256,128]{4,2,0,1,3:T(2,128)(2,1)S(1)}, u32[]{:S(2)}, u32[]{:S(2)}) async-start(bf16[8,1,2,256,128]{4,2,0,1,3:T(2,128)(2,1)} %bitcast.448), calls=%async_computation.34 | async-start | bytes 2097152 | tf_op jit(solution)/shard_map/all_to_all | solution.py:151
  741.9 234.2 %all-reduce.2.cloned.1.call-start = ((), (), s32[]{:S(2)}) async-start(), calls=%async_computation.38 | async-start | bytes 524288 | tf_op jit(solution)/shard_map/psum | solution.py:177
  (47 other events, 1802.5 us)
Sparse Core Ops, SparseCore 0:
  668.1 240.8 reduce-scatter.1
  911.3 64.7 all-reduce.1
where the time goes:
time: 997 us; the launch traced here: 985 us
  waiting for transfers between devices  383 us (38%)
  blocking collectives  233 us (23%)
  starting transfers between devices  171 us (17%)
  matrix products  89.7 us (9%)
  local copies, waits for them, and re-layouts  73 us (7%)
  other arithmetic  20 us (2%)
  between operations  15.2 us (2%)
    reduce_scatter x1, waiting for transfers between devices, per_device(): lax.psum_scatter(lax.dot_general(attn_out, cotangent, (((0,), (0,)), ((),...  138 us
    all_to_all x6, blocking collectives, per_device(): lax.all_to_all(grad_slots[head_index], 'ctx', split_axis=0, concat_axis=2...  91.4 us
    psum x1, waiting for transfers between devices, per_device(): wo_grad = lax.psum(shard_sum, 'dp')  60.9 us
    all_to_all x8, waiting for transfers between devices, per_device(): lax.all_to_all(query_slots[head_index], 'ctx', split_axis=0, concat_axis=...  59.1 us
    all_to_all x8, starting transfers between devices, per_device(): lax.all_to_all(key_slots[head_index], 'ctx', split_axis=0, concat_axis=2,...  53.1 us
    all_to_all x8, starting transfers between devices, per_device(): lax.all_to_all(value_slots[head_index], 'ctx', split_axis=0, concat_axis=...  52.8 us
    all_to_all x8, starting transfers between devices, per_device(): lax.all_to_all(query_slots[head_index], 'ctx', split_axis=0, concat_axis=...  48.7 us
    all_to_all x8, waiting for transfers between devices, per_device(): lax.all_to_all(key_slots[head_index], 'ctx', split_axis=0, concat_axis=2,...  47.1 us
  transfers between devices with their start and end apart: 29, of which 26 were waited for; matrix products, arithmetic and copies ran while one was open for 8% of the time, Pallas kernels for 0%

commit v1 on v0

--- a/solution.py
+++ b/solution.py
@@ -174,7 +174,7 @@
         scatter_dimension=0,
         tiled=True,
     )
-    wo_grad = lax.psum(shard_sum, "dp")
+    wo_grad = jnp.sum(lax.all_gather(shard_sum, "dp"), axis=0)
     return (layer_out, q_grad, k_grad, v_grad, wo_grad)
 
 

time: 997 us -> 964 us (0.967)
  blocking collectives: 233 us -> 193 us
    reduce_scatter x1, waiting for transfers between devices: 138 us -> 199 us  [per_device(): lax.psum_scatter(lax.dot_general(attn_out, cotangent, (((0,), (0,)), ((),...]
    psum x1 -> x0, waiting for transfers between devices: 60.9 us -> none  [per_device(): wo_grad = lax.psum(shard_sum, 'dp')]
    all_to_all x1 -> x0, blocking collectives: 28.6 us -> none  [per_device(): lax.all_to_all(owner_view(query_grad), 'ctx', split_axis=3, concat_axis=1...]
    unnamed x87 -> x80, local copies, waits for them, and re-layouts: 37.4 us -> 35.3 us
  transfers between devices with their start and end apart: 29 -> 30, of which waited for: 26 -> 25; matrix products, arithmetic and copies ran while one was open for 8% -> 8% of each run, Pallas kernels for 0% -> 0%
where the time goes in v1:
time: 964 us; the launch traced here: 952 us
  waiting for transfers between devices  382 us (40%)
  blocking collectives  193 us (20%)
  starting transfers between devices  179 us (19%)
  matrix products  91.1 us (9%)
  local copies, waits for them, and re-layouts  68.5 us (7%)
  other arithmetic  22.4 us (2%)
  between operations  15.2 us (2%)
    reduce_scatter x1, waiting for transfers between devices, per_device(): lax.psum_scatter(lax.dot_general(attn_out, cotangent, (((0,), (0,)), ((),...  199 us
    all_to_all x6, blocking collectives, per_device(): lax.all_to_all(grad_slots[head_index], 'ctx', split_axis=0, concat_axis=2...  91.4 us
    all_to_all x8, waiting for transfers between devices, per_device(): lax.all_to_all(query_slots[head_index], 'ctx', split_axis=0, concat_axis=...  59 us
    all_to_all x8, starting transfers between devices, per_device(): lax.all_to_all(key_slots[head_index], 'ctx', split_axis=0, concat_axis=2,...  53.1 us
    all_to_all x8, starting transfers between devices, per_device(): lax.all_to_all(value_slots[head_index], 'ctx', split_axis=0, concat_axis=...  52.8 us
    all_to_all x8, starting transfers between devices, per_device(): lax.all_to_all(query_slots[head_index], 'ctx', split_axis=0, concat_axis=...  48.8 us
    all_to_all x8, waiting for transfers between devices, per_device(): lax.all_to_all(key_slots[head_index], 'ctx', split_axis=0, concat_axis=2,...  47 us
    all_gather x1, blocking collectives, per_device(): every_ids = lax.all_gather(cluster_ids, 'ctx', axis=1, tiled=True)  43.9 us
  transfers between devices with their start and end apart: 30, of which 25 were waited for; matrix products, arithmetic and copies ran while one was open for 8% of the time, Pallas kernels for 0%

profile of v1, /device:TPU:2, one launch (start us, length us, event | category | flops | bytes accessed | tf_op | source)
XLA Modules:
  0.0 952.3 jit_solution(3484231713567655390)
XLA Ops:
  15.1 20.5 %all_to_all.540 = bf16[32,2,8,128]{3,2,1,0:T(8,128)(2,1)} all-to-all(bf16[32,2,8,128]{3,2,1,0:T(8,128)(2,1)S(1)} %bitcast.465), channel_id=1, replica_groups=mesh['dp'=8,'ctx'=32] {'ctx'}, dimensions={0} | all-to-all | bytes 262144 | tf_op jit(solution)/shard_map/all_to_all | solution.py:96
  35.6 14.1 %all_to_all.541 = bf16[32,2,8,128]{3,2,1,0:T(8,128)(2,1)} all-to-all(bf16[32,2,8,128]{3,2,1,0:T(8,128)(2,1)S(1)} %bitcast.463), channel_id=1, replica_groups=mesh['dp'=8,'ctx'=32] {'ctx'}, dimensions={0} | all-to-all | bytes 262144 | tf_op jit(solution)/shard_map/all_to_all | solution.py:96
  49.7 14.3 %all_to_all.542 = bf16[32,2,8,128]{3,2,1,0:T(8,128)(2,1)} all-to-all(bf16[32,2,8,128]{3,2,1,0:T(8,128)(2,1)S(1)} %bitcast.462), channel_id=1, replica_groups=mesh['dp'=8,'ctx'=32] {'ctx'}, dimensions={0} | all-to-all | bytes 262144 | tf_op jit(solution)/shard_map/all_to_all | solution.py:96
  64.0 14.2 %all_to_all.543 = bf16[32,2,8,128]{3,2,1,0:T(8,128)(2,1)} all-to-all(bf16[32,2,8,128]{3,2,1,0:T(8,128)(2,1)S(1)} %bitcast.461), channel_id=1, replica_groups=mesh['dp'=8,'ctx'=32] {'ctx'}, dimensions={0} | all-to-all | bytes 262144 | tf_op jit(solution)/shard_map/all_to_all | solution.py:96
  78.1 14.2 %all_to_all.544 = bf16[32,2,8,128]{3,2,1,0:T(8,128)(2,1)} all-to-all(bf16[32,2,8,128]{3,2,1,0:T(8,128)(2,1)S(1)} %bitcast.460), channel_id=1, replica_groups=mesh['dp'=8,'ctx'=32] {'ctx'}, dimensions={0} | all-to-all | bytes 262144 | tf_op jit(solution)/shard_map/all_to_all | solution.py:96
  92.3 14.2 %all_to_all.545 = bf16[32,2,8,128]{3,2,1,0:T(8,128)(2,1)} all-to-all(bf16[32,2,8,128]{3,2,1,0:T(8,128)(2,1)S(1)} %bitcast.459), channel_id=1, replica_groups=mesh['dp'=8,'ctx'=32] {'ctx'}, dimensions={0} | all-to-all | bytes 262144 | tf_op jit(solution)/shard_map/all_to_all | solution.py:96
  127.4 8.0 all-to-all-done.24
  140.9 43.9 %all_gather.9 = s32[8,8192,1]{1,2,0:T(1,128)S(1)} all-gather(s32[8,256,1]{1,2,0:T(1,128)S(1)} %copy-done.18), channel_id=1, replica_groups=mesh['dp'=8,'ctx'=32] {'ctx'}, dimensions={1}, use_global_device_ids=true | all-gather | bytes 270336 | tf_op jit(solution)/shard_map/all_gather | solution.py:106
  185.5 8.7 all-to-all-start.23
  195.3 7.7 all-to-all-done.23
  209.5 9.1 select_reduce_fusion
  218.6 9.9 %all-to-all-start.20 = ((bf16[32,2,8,128]{3,2,1,0:T(8,128)(2,1)}), bf16[32,2,8,128]{3,2,1,0:T(8,128)(2,1)S(1)}, u32[]{:S(2)}, u32[]{:S(2)}) async-start(bf16[32,2,8,128]{3,2,1,0:T(8,128)(2,1)} %bitcast.99), calls=%async_computation.20 | async-start | bytes 262144 | tf_op jit(solution)/shard_map/all_to_all | solution.py:93
  228.7 8.7 all-to-all-done.20
  288.3 8.0 all-to-all-done.16
  296.4 14.8 %all-to-all-start.8 = ((bf16[32,2,8,128]{3,2,1,0:T(8,128)(2,1)}), bf16[32,2,8,128]{3,2,1,0:T(8,128)(2,1)}, u32[]{:S(2)}, u32[]{:S(2)}) async-start(bf16[32,2,8,128]{3,2,1,0:T(8,128)(2,1)} %bitcast.50), calls=%async_computation.8 | async-start | bytes 262144 | tf_op jit(solution)/shard_map/all_to_all | solution.py:90
  311.2 9.1 fusion.71
  322.9 9.9 %all-to-all-start = ((bf16[32,2,8,128]{3,2,1,0:T(8,128)(2,1)}), bf16[32,2,8,128]{3,2,1,0:T(8,128)(2,1)S(1)}, u32[]{:S(2)}, u32[]{:S(2)}) async-start(bf16[32,2,8,128]{3,2,1,0:T(8,128)(2,1)} %bitcast.17), calls=%async_computation | async-start | bytes 262144 | tf_op jit(solution)/shard_map/all_to_all | solution.py:87
  478.9 8.4 all-to-all-done.2
  545.9 85.3 %while.18 = (s32[]{:T(128)}, bf16[8,2,256,128]{3,1,0,2:T(2,128)(2,1)S(1)}, bf16[8,2,256,128]{3,1,0,2:T(2,128)(2,1)}, bf16[8,2,256,128]{3,1,0,2:T(2,128)(2,1)}, b...) while((s32[]{:T(128)}, ...), condition=%wide.region_7.8_spmd, body=%wide.region_3.7_spmd.sunk | while | flops 205137152 | bytes 11052245 | solution.py:133
  631.3 27.5 %all_to_all.546 = bf16[8,1,2,256,128]{4,2,0,1,3:T(2,128)(2,1)S(1)} all-to-all(bf16[8,1,2,256,128]{4,2,0,1,3:T(2,128)(2,1)S(1)} %bitcast.452), channel_id=1, replica_groups=mesh['dp'=8,'ctx'=32] {'ctx'}, dimensions={3} | all-to-all | bytes 2097152 | tf_op jit(solution)/shard_map/all_to_all | solution.py:149
  667.2 30.3 %all_to_all.547 = bf16[8,1,2,256,128]{4,2,0,1,3:T(2,128)(2,1)S(1)} all-to-all(bf16[8,1,2,256,128]{4,2,0,1,3:T(2,128)(2,1)S(1)} %bitcast.449), channel_id=1, replica_groups=mesh['dp'=8,'ctx'=32] {'ctx'}, dimensions={3} | all-to-all | bytes 2097152 | tf_op jit(solution)/shard_map/all_to_all | solution.py:152
  702.6 198.8 %reduce-scatter.2.cloned.1.call-done = f32[32,2048]{1,0:T(8,128)} async-done(((f32[1024,2048]{1,0:T(8,128)}), f32[32,2048]{1,0:T(8,128)}) %reduce-scatter.2.cloned.1.call-update) | async-done | bytes 262160 | tf_op jit(solution)/shard_map/reduce_scatter | solution.py:168
  901.4 8.6 all-to-all-start.34
  915.7 18.4 %all-to-all-done.34 = bf16[8,1,2,256,128]{4,2,0,1,3:T(2,128)(2,1)} async-done(((bf16[8,1,2,256,128]{4,2,0,1,3:T(2,128)(2,1)}), bf16[8,1,2,256,128]{4,2,0,1,3:T(2,128)(2,1)}, u32[]{:S(2)}, u32[]{:S(2)}) %all-to-all-start.34) | async-done | bytes 1048608 | tf_op jit(solution)/shard_map/all_to_all | solution.py:151
  (289 shorter events, 415.4 us)
Async XLA Ops:
  106.5 14.4 %all-to-all-start.25 = ((bf16[32,2,8,128]{3,2,1,0:T(8,128)(2,1)}), bf16[32,2,8,128]{3,2,1,0:T(8,128)(2,1)S(1)}, u32[]{:S(2)}, u32[]{:S(2)}) async-start(bf16[32,2,8,128]{3,2,1,0:T(8,128)(2,1)} %bitcast.120), calls=%async_computation.25 | async-start | bytes 262144 | tf_op jit(solution)/shard_map/all_to_all | solution.py:96
  121.0 14.4 %all-to-all-start.24 = ((bf16[32,2,8,128]{3,2,1,0:T(8,128)(2,1)}), bf16[32,2,8,128]{3,2,1,0:T(8,128)(2,1)S(1)}, u32[]{:S(2)}, u32[]{:S(2)}) async-start(bf16[32,2,8,128]{3,2,1,0:T(8,128)(2,1)} %bitcast.116), calls=%async_computation.24 | async-start | bytes 262144 | tf_op jit(solution)/shard_map/all_to_all | solution.py:96
  135.4 50.1 %all-to-all-start.22 = ((bf16[32,2,8,128]{3,2,1,0:T(8,128)(2,1)}), bf16[32,2,8,128]{3,2,1,0:T(8,128)(2,1)S(1)}, u32[]{:S(2)}, u32[]{:S(2)}) async-start(bf16[32,2,8,128]{3,2,1,0:T(8,128)(2,1)} %bitcast.107), calls=%async_computation.22 | async-start | bytes 262144 | tf_op jit(solution)/shard_map/all_to_all | solution.py:93
  185.5 17.5 %all-to-all-start.23 = ((bf16[32,2,8,128]{3,2,1,0:T(8,128)(2,1)}), bf16[32,2,8,128]{3,2,1,0:T(8,128)(2,1)S(1)}, u32[]{:S(2)}, u32[]{:S(2)}) async-start(bf16[32,2,8,128]{3,2,1,0:T(8,128)(2,1)} %bitcast.111), calls=%async_computation.23 | async-start | bytes 262144 | tf_op jit(solution)/shard_map/all_to_all | solution.py:93
  203.7 14.9 %all-to-all-start.21 = ((bf16[32,2,8,128]{3,2,1,0:T(8,128)(2,1)}), bf16[32,2,8,128]{3,2,1,0:T(8,128)(2,1)S(1)}, u32[]{:S(2)}, u32[]{:S(2)}) async-start(bf16[32,2,8,128]{3,2,1,0:T(8,128)(2,1)} %bitcast.103), calls=%async_computation.21 | async-start | bytes 262144 | tf_op jit(solution)/shard_map/all_to_all | solution.py:93
  218.6 18.8 %all-to-all-start.20 = ((bf16[32,2,8,128]{3,2,1,0:T(8,128)(2,1)}), bf16[32,2,8,128]{3,2,1,0:T(8,128)(2,1)S(1)}, u32[]{:S(2)}, u32[]{:S(2)}) async-start(bf16[32,2,8,128]{3,2,1,0:T(8,128)(2,1)} %bitcast.99), calls=%async_computation.20 | async-start | bytes 262144 | tf_op jit(solution)/shard_map/all_to_all | solution.py:93
  251.7 14.4 %all-to-all-start.18 = ((bf16[32,2,8,128]{3,2,1,0:T(8,128)(2,1)}), bf16[32,2,8,128]{3,2,1,0:T(8,128)(2,1)S(1)}, u32[]{:S(2)}, u32[]{:S(2)}) async-start(bf16[32,2,8,128]{3,2,1,0:T(8,128)(2,1)} %bitcast.91), calls=%async_computation.18 | async-start | bytes 262144 | tf_op jit(solution)/shard_map/all_to_all | solution.py:93
  266.1 15.1 %all-to-all-start.17 = ((bf16[32,2,8,128]{3,2,1,0:T(8,128)(2,1)}), bf16[32,2,8,128]{3,2,1,0:T(8,128)(2,1)}, u32[]{:S(2)}, u32[]{:S(2)}) async-start(bf16[32,2,8,128]{3,2,1,0:T(8,128)(2,1)} %bitcast.87), calls=%async_computation.17 | async-start | bytes 262144 | tf_op jit(solution)/shard_map/all_to_all | solution.py:93
  281.2 15.1 %all-to-all-start.16 = ((bf16[32,2,8,128]{3,2,1,0:T(8,128)(2,1)}), bf16[32,2,8,128]{3,2,1,0:T(8,128)(2,1)}, u32[]{:S(2)}, u32[]{:S(2)}) async-start(bf16[32,2,8,128]{3,2,1,0:T(8,128)(2,1)} %bitcast.83), calls=%async_computation.16 | async-start | bytes 262144 | tf_op jit(solution)/shard_map/all_to_all | solution.py:93
  296.4 26.5 %all-to-all-start.8 = ((bf16[32,2,8,128]{3,2,1,0:T(8,128)(2,1)}), bf16[32,2,8,128]{3,2,1,0:T(8,128)(2,1)}, u32[]{:S(2)}, u32[]{:S(2)}) async-start(bf16[32,2,8,128]{3,2,1,0:T(8,128)(2,1)} %bitcast.50), calls=%async_computation.8 | async-start | bytes 262144 | tf_op jit(solution)/shard_map/all_to_all | solution.py:90
  322.9 18.8 %all-to-all-start = ((bf16[32,2,8,128]{3,2,1,0:T(8,128)(2,1)}), bf16[32,2,8,128]{3,2,1,0:T(8,128)(2,1)S(1)}, u32[]{:S(2)}, u32[]{:S(2)}) async-start(bf16[32,2,8,128]{3,2,1,0:T(8,128)(2,1)} %bitcast.17), calls=%async_computation | async-start | bytes 262144 | tf_op jit(solution)/shard_map/all_to_all | solution.py:87
  341.7 14.5 %all-to-all-start.14 = ((bf16[32,2,8,128]{3,2,1,0:T(8,128)(2,1)}), bf16[32,2,8,128]{3,2,1,0:T(8,128)(2,1)S(1)}, u32[]{:S(2)}, u32[]{:S(2)}) async-start(bf16[32,2,8,128]{3,2,1,0:T(8,128)(2,1)} %bitcast.74), calls=%async_computation.14 | async-start | bytes 262144 | tf_op jit(solution)/shard_map/all_to_all | solution.py:90
  384.9 14.6 %all-to-all-start.12 = ((bf16[32,2,8,128]{3,2,1,0:T(8,128)(2,1)}), bf16[32,2,8,128]{3,2,1,0:T(8,128)(2,1)S(1)}, u32[]{:S(2)}, u32[]{:S(2)}) async-start(bf16[32,2,8,128]{3,2,1,0:T(8,128)(2,1)} %bitcast.66), calls=%async_computation.12 | async-start | bytes 262144 | tf_op jit(solution)/shard_map/all_to_all | solution.py:90
  428.4 14.4 %all-to-all-start.9 = ((bf16[32,2,8,128]{3,2,1,0:T(8,128)(2,1)}), bf16[32,2,8,128]{3,2,1,0:T(8,128)(2,1)S(1)}, u32[]{:S(2)}, u32[]{:S(2)}) async-start(bf16[32,2,8,128]{3,2,1,0:T(8,128)(2,1)} %bitcast.54), calls=%async_computation.9 | async-start | bytes 262144 | tf_op jit(solution)/shard_map/all_to_all | solution.py:90
  457.2 14.5 %all-to-all-start.4 = ((bf16[32,2,8,128]{3,2,1,0:T(8,128)(2,1)}), bf16[32,2,8,128]{3,2,1,0:T(8,128)(2,1)S(1)}, u32[]{:S(2)}, u32[]{:S(2)}) async-start(bf16[32,2,8,128]{3,2,1,0:T(8,128)(2,1)} %bitcast.33), calls=%async_computation.4 | async-start | bytes 262144 | tf_op jit(solution)/shard_map/all_to_all | solution.py:87
  471.7 15.5 %all-to-all-start.2 = ((bf16[32,2,8,128]{3,2,1,0:T(8,128)(2,1)}), bf16[32,2,8,128]{3,2,1,0:T(8,128)(2,1)S(1)}, u32[]{:S(2)}, u32[]{:S(2)}) async-start(bf16[32,2,8,128]{3,2,1,0:T(8,128)(2,1)} %bitcast.25), calls=%async_computation.2 | async-start | bytes 262144 | tf_op jit(solution)/shard_map/all_to_all | solution.py:87
  487.3 14.7 %all-to-all-start.1 = ((bf16[32,2,8,128]{3,2,1,0:T(8,128)(2,1)}), bf16[32,2,8,128]{3,2,1,0:T(8,128)(2,1)S(1)}, u32[]{:S(2)}, u32[]{:S(2)}) async-start(bf16[32,2,8,128]{3,2,1,0:T(8,128)(2,1)} %bitcast.21), calls=%async_computation.1 | async-start | bytes 262144 | tf_op jit(solution)/shard_map/all_to_all | solution.py:87
  502.0 14.4 %all-to-all-start.3 = ((bf16[32,2,8,128]{3,2,1,0:T(8,128)(2,1)}), bf16[32,2,8,128]{3,2,1,0:T(8,128)(2,1)S(1)}, u32[]{:S(2)}, u32[]{:S(2)}) async-start(bf16[32,2,8,128]{3,2,1,0:T(8,128)(2,1)} %bitcast.29), calls=%async_computation.3 | async-start | bytes 262144 | tf_op jit(solution)/shard_map/all_to_all | solution.py:87
  516.4 14.4 %all-to-all-start.5 = ((bf16[32,2,8,128]{3,2,1,0:T(8,128)(2,1)}), bf16[32,2,8,128]{3,2,1,0:T(8,128)(2,1)S(1)}, u32[]{:S(2)}, u32[]{:S(2)}) async-start(bf16[32,2,8,128]{3,2,1,0:T(8,128)(2,1)} %bitcast.37), calls=%async_computation.5 | async-start | bytes 262144 | tf_op jit(solution)/shard_map/all_to_all | solution.py:87
  530.9 14.4 %all-to-all-start.7 = ((bf16[32,2,8,128]{3,2,1,0:T(8,128)(2,1)}), bf16[32,2,8,128]{3,2,1,0:T(8,128)(2,1)S(1)}, u32[]{:S(2)}, u32[]{:S(2)}) async-start(bf16[32,2,8,128]{3,2,1,0:T(8,128)(2,1)} %bitcast.45), calls=%async_computation.7 | async-start | bytes 262144 | tf_op jit(solution)/shard_map/all_to_all | solution.py:87
  536.3 365.1 %reduce-scatter.2.cloned.1.call-start = ((), (), s32[]{:S(2)}) async-start(), calls=%async_computation.37 | async-start | bytes 8650752 | tf_op jit(solution)/shard_map/reduce_scatter | solution.py:168
  697.5 203.9 %all-to-all-start.33 = ((bf16[8,1,2,256,128]{4,2,0,1,3:T(2,128)(2,1)}), bf16[8,1,2,256,128]{4,2,0,1,3:T(2,128)(2,1)S(1)}, u32[]{:S(2)}, u32[]{:S(2)}) async-start(bf16[8,1,2,256,128]{4,2,0,1,3:T(2,128)(2,1)} %bitcast.451), calls=%async_computation.33 | async-start | bytes 2097152 | tf_op jit(solution)/shard_map/all_to_all | solution.py:150
  702.6 240.1 %all-gather.3.cloned.1.call-start = ((), (), s32[]{:S(2)}) async-start(), calls=%async_computation.38 | async-start | bytes 2359296 | tf_op jit(solution)/shard_map/all_gather | solution.py:177
  901.4 32.7 %all-to-all-start.34 = ((bf16[8,1,2,256,128]{4,2,0,1,3:T(2,128)(2,1)}), bf16[8,1,2,256,128]{4,2,0,1,3:T(2,128)(2,1)}, u32[]{:S(2)}, u32[]{:S(2)}) async-start(bf16[8,1,2,256,128]{4,2,0,1,3:T(2,128)(2,1)} %bitcast.450), calls=%async_computation.34 | async-start | bytes 2097152 | tf_op jit(solution)/shard_map/all_to_all | solution.py:151
  (45 other events, 1797.3 us)
Sparse Core Ops, SparseCore 0:
  666.1 235.2 reduce-scatter.1
  903.3 27.0 all-gather.2
